TPU v7x, 256 devices: a whole 4x4x8 slice. The times are simulated.
256 devices in a mesh: gx: 32 (over y_hi, z, core), gy: 8 (over y_lo, x).
Axes of the slice: x: 4, y: 4 (y_hi: 2, y_lo: 2; y = y_hi * 2 + y_lo), z: 8, core: 2. Of those that a mesh axis runs over, the one named last changes fastest.
Arguments:
- state_field: bfloat16 [1, 64, 2048, 2048], P(None, None, 'gx', 'gy'), may hold values from -6 to 6
- spectral_x: bfloat16 [2, 32, 2, 64, 64], P(None, 'gx'), may hold values from -2 to 2
- spectral_y: bfloat16 [2, 32, 2, 64, 64], P(None, 'gy'), may hold values from -2 to 2
- expand_weight: bfloat16 [2, 64, 256], replicated, may hold values from -0.75 to 0.75
- reduce_weight: bfloat16 [2, 256, 64], replicated, may hold values from -0.375 to 0.375
Outputs:
- next_state: bfloat16 [1, 64, 2048, 2048], P(None, None, 'gx', 'gy')
All inputs are finite; a program needn't handle non-finite values.
Results may differ from a plain program's by a relative error of at most 0.025.
Values may be sent and summed in bfloat16 or wider, within the bound.
No kernel may reach another device: no remote copies, remote signals or barrier semaphores. Data moves between devices by JAX's collectives and lax.ppermute only.
A program may use at most 64 MiB of HBM per device.

v0:
```python
import jax
import jax.numpy as jnp
from jax import lax
from jax.sharding import PartitionSpec as P

NX = 2048
NY = 2048
MODES = 32
LAYERS = 2


def make_tables(length, modes):
    positions = jnp.arange(length, dtype=jnp.int32)
    orders = jnp.arange(modes, dtype=jnp.int32)
    phase = orders[:, None] * positions[None, :] % length
    angle = 2.0 * jnp.pi * phase.astype(jnp.float32) / length
    factor = 1.0 / jnp.sqrt(jnp.float32(length))
    weight_two = jnp.where(orders == 0, 1.0, 2.0).astype(jnp.float32)[:, None]
    forward = jnp.stack([jnp.cos(angle) * factor, -jnp.sin(angle) * factor], axis=1)
    forward = forward.reshape(2 * modes, length).astype(jnp.bfloat16)
    inverse = jnp.stack(
        [weight_two * jnp.cos(angle) * factor, -weight_two * jnp.sin(angle) * factor], axis=1
    )
    inverse = inverse.reshape(2 * modes, length).T.astype(jnp.bfloat16)
    return (forward, inverse)


def mix_modes(spectrum, weights):
    modes = weights.shape[0]
    shaped = spectrum.reshape((modes, 2) + spectrum.shape[1:])
    real_in, imag_in = (shaped[:, 0], shaped[:, 1])
    real_w, imag_w = (weights[:, 0], weights[:, 1])

    def contract_modes(left, right):
        return jnp.einsum("koi,kzin->kzon", left, right, preferred_element_type=jnp.float32)

    real_out = contract_modes(real_w, real_in) - contract_modes(imag_w, imag_in)
    imag_out = contract_modes(real_w, imag_in) + contract_modes(imag_w, real_in)
    joined = jnp.stack([real_out, imag_out], axis=1).astype(jnp.bfloat16)
    return joined.reshape(spectrum.shape)


def body(state_field, spectral_x, spectral_y, expand_weight, reduce_weight):
    planes, channels, local_rows, local_cols = state_field.shape
    row_first = lax.axis_index("gx") * local_rows
    col_first = lax.axis_index("gy") * local_cols
    forward_x, inverse_x = make_tables(NX, MODES)
    forward_y, inverse_y = make_tables(NY, MODES)
    forward_xloc = lax.dynamic_slice_in_dim(forward_x, row_first, local_rows, 1)
    inverse_xloc = lax.dynamic_slice_in_dim(inverse_x, row_first, local_rows, 0)
    forward_yloc = lax.dynamic_slice_in_dim(forward_y, col_first, local_cols, 1)
    inverse_yloc = lax.dynamic_slice_in_dim(inverse_y, col_first, local_cols, 0)
    state = state_field
    for layer_index in range(LAYERS):
        weights_x = spectral_x[layer_index]
        weights_y = spectral_y[layer_index]
        spec_x = lax.psum_scatter(
            jnp.einsum(
                "kx,zcxy->kzcy", forward_xloc, state, preferred_element_type=jnp.float32
            ).astype(jnp.bfloat16),
            "gx",
            scatter_dimension=0,
            tiled=True,
        )
        spec_y = lax.psum_scatter(
            jnp.einsum(
                "ky,zcxy->kzcx", forward_yloc, state, preferred_element_type=jnp.float32
            ).astype(jnp.bfloat16),
            "gy",
            scatter_dimension=0,
            tiled=True,
        )
        mixed_x = mix_modes(spec_x, weights_x)
        mixed_y = mix_modes(spec_y, weights_y)
        branch_x = jnp.einsum(
            "xk,kzcy->zcxy",
            inverse_xloc,
            lax.all_gather(mixed_x, "gx", axis=0, tiled=True),
            preferred_element_type=jnp.float32,
        ).astype(jnp.bfloat16)
        branch_y = jnp.einsum(
            "yk,kzcx->zcxy",
            inverse_yloc,
            lax.all_gather(mixed_y, "gy", axis=0, tiled=True),
            preferred_element_type=jnp.float32,
        ).astype(jnp.bfloat16)
        total = (branch_x.astype(jnp.float32) + branch_y.astype(jnp.float32)).astype(jnp.bfloat16)
        hidden = jax.nn.gelu(
            jnp.einsum(
                "ch,zcxy->zhxy",
                expand_weight[layer_index],
                total,
                preferred_element_type=jnp.float32,
            ),
            approximate=True,
        )
        hidden = hidden.astype(jnp.bfloat16)
        update = jnp.einsum(
            "hc,zhxy->zcxy", reduce_weight[layer_index], hidden, preferred_element_type=jnp.float32
        )
        state = (state.astype(jnp.float32) + update).astype(jnp.bfloat16)
    return state


def solution(mesh):
    in_specs = (
        P(None, None, "gx", "gy"),
        P(None, "gx", None, None, None),
        P(None, "gy", None, None, None),
        P(),
        P(),
    )
    out_specs = P(None, None, "gx", "gy")
    return jax.shard_map(body, mesh=mesh, in_specs=in_specs, out_specs=out_specs, check_vma=False)
```

profile of v0, /device:TPU:1, one launch (start us, length us, event | category | flops | bytes accessed | tf_op | source)
XLA Modules:
  0.0 543.5 jit_solution(1677750337479074670)
XLA Ops:
  6.5 1.1 multiply_convert_fusion.2
  7.7 0.3 copy.123
  8.1 2.3 convert_bitcast_fusion.3
  10.4 2.5 copy.124
  13.0 1.5 copy-done
  14.5 1.1 fusion.63
  15.6 0.7 copy.153
  16.3 1.6 reshape.480
  18.0 0.6 slice_bitcast_fusion.28
  18.6 112.1 %reduce-scatter.9.cloned.1.call-done = bf16[2,1,64,256]{3,2,1,0:T(8,128)(2,1)} async-done(((bf16[64,1,64,256]{3,2,1,0:T(8,128)(2,1)}), bf16[2,1,64,256]{3,2,1,0:T(8,128)(2,1)}) %reduce-scatter.9.cloned.1.call-update) | async-done | bytes 65552 | tf_op jit(solution)/shard_map/reduce_scatter | solution.py:57
  130.7 0.9 fusion.118
  131.6 0.9 fusion.83
  132.5 0.9 fusion.117
  133.4 0.9 fusion.84
  134.3 0.6 pad_maximum_fusion.4
  135.1 1.0 multiply_convert_fusion
  136.1 1.0 multiply_convert_fusion.1
  137.1 0.3 copy.126
  137.4 0.8 convert_element_type.187
  138.2 33.9 %reduce-scatter.13.cloned.1.call-done = bf16[8,4096]{1,0:T(8,128)(2,1)} async-done(((bf16[64,4096]{1,0:T(8,128)(2,1)}), bf16[8,4096]{1,0:T(8,128)(2,1)}) %reduce-scatter.13.cloned.1.call-update) | async-done | bytes 65552
  172.1 1.0 reshape.481
  174.1 24.2 %all_gather.13 = bf16[64,1,64,64]{3,2,1,0:T(8,128)(2,1)S(1)} all-gather(bf16[8,1,64,64]{3,2,1,0:T(8,128)(2,1)S(1)} %bitcast.306), channel_id=1, replica_groups=mesh['gx'=32,'gy'=8] {'gy'}, dimensions={0}, use_global_device_ids=true | all-gather | bytes 589824 | tf_op jit(solution)/shard_map/all_gather | solution.py:84
  198.3 1.2 copy.134
  199.5 1.4 fusion.87
  201.0 58.1 %all-gather.3.cloned.1.call-done = bf16[64,1,64,256]{3,2,1,0:T(8,128)(2,1)} async-done(((bf16[2,1,64,256]{3,2,1,0:T(8,128)(2,1)}), bf16[64,1,64,256]{3,2,1,0:T(8,128)(2,1)}) %all-gather.3.cloned.1.call-update) | async-done | bytes 2097168 | tf_op jit(solution)/shard_map/all_gather | solution.py:78
  259.1 4.7 fusion.24
  263.9 12.2 %fusion.22 = bf16[1,64,64,256]{3,1,2,0:T(8,128)(2,1)S(1)} fusion(bf16[1,64,64,256]{3,2,1,0:T(8,128)(2,1)} %param.5, bf16[64,64,256]{2,1,0:T(8,128)(2,1)} %fusion.24, bf16[2,256,64]{1,2,0:T(8,128)(2,1)S(1)} %copy-done.5, bf16[2,64,256]{2,1,0:T(8,128)(2,1)S(1)} %copy-done.7), kind=kOutput, calls=%fused_computation.28 | convolution fusion | flops 1114636288 | bytes 6356992 | tf_op jit(solution)/shard_map/hc,zhxy->zcxy/dot_general | solution.py:98
  276.1 1.7 convert_bitcast_fusion.2
  277.9 2.5 copy.138
  280.4 0.3 reduce-scatter.15.cloned.1.call-start
  280.7 2.6 fusion.66
  283.3 0.7 copy.155
  284.0 1.6 reshape.482
  285.7 105.2 %reduce-scatter.11.cloned.1.call-done = bf16[2,1,64,256]{3,2,1,0:T(8,128)(2,1)} async-done(((bf16[64,1,64,256]{3,2,1,0:T(8,128)(2,1)}), bf16[2,1,64,256]{3,2,1,0:T(8,128)(2,1)}) %reduce-scatter.11.cloned.1.call-update) | async-done | bytes 65552 | tf_op jit(solution)/shard_map/reduce_scatter | solution.py:57
  390.9 0.9 fusion.119
  391.7 0.9 fusion.82
  392.6 0.9 fusion.120
  393.5 0.9 fusion.81
  394.4 0.6 pad_maximum_fusion.5
  395.1 36.6 %reduce-scatter.15.cloned.1.call-done = bf16[8,4096]{1,0:T(8,128)(2,1)} async-done(((bf16[64,4096]{1,0:T(8,128)(2,1)}), bf16[8,4096]{1,0:T(8,128)(2,1)}) %reduce-scatter.15.cloned.1.call-update) | async-done | bytes 65552
  431.7 1.0 reshape.483
  433.8 24.0 %all_gather.15 = bf16[64,1,64,64]{3,2,1,0:T(8,128)(2,1)S(1)} all-gather(bf16[8,1,64,64]{3,2,1,0:T(8,128)(2,1)S(1)} %bitcast.307), channel_id=1, replica_groups=mesh['gx'=32,'gy'=8] {'gy'}, dimensions={0}, use_global_device_ids=true | all-gather | bytes 589824 | tf_op jit(solution)/shard_map/all_gather | solution.py:84
  457.8 1.2 copy.147
  459.0 1.4 fusion.85
  460.5 58.2 %all-gather.5.cloned.1.call-done = bf16[64,1,64,256]{3,2,1,0:T(8,128)(2,1)} async-done(((bf16[2,1,64,256]{3,2,1,0:T(8,128)(2,1)}), bf16[64,1,64,256]{3,2,1,0:T(8,128)(2,1)}) %all-gather.5.cloned.1.call-update) | async-done | bytes 2097168 | tf_op jit(solution)/shard_map/all_gather | solution.py:78
  518.7 4.7 fusion.25
  523.4 10.8 %fusion.20 = bf16[1,64,64,256]{3,1,2,0:T(8,128)(2,1)S(1)} fusion(bf16[1,64,64,256]{3,1,2,0:T(8,128)(2,1)} %copy-done.1, bf16[64,64,256]{2,1,0:T(8,128)(2,1)} %fusion.25, bf16[2,256,64]{1,2,0:T(8,128)(2,1)S(1)} %copy-done.6, bf16[2,64,256]{2,1,0:T(8,128)(2,1)S(1)} %copy-done.8), kind=kOutput, calls=%fused_computation.23 | convolution fusion | flops 1114636288 | bytes 6356992 | tf_op jit(solution)/shard_map/hc,zhxy->zcxy/dot_general | solution.py:98
  534.2 2.5 copy.150
  (47 shorter events, 2.5 us)
Async XLA Ops:
  6.5 124.2 %reduce-scatter.9.cloned.1.call-start = ((), (), s32[]{:S(2)}) async-start(), calls=%async_computation.4 | async-start | bytes 2162688 | tf_op jit(solution)/shard_map/reduce_scatter | solution.py:57
  12.9 1.6 copy-start
  12.9 159.1 %reduce-scatter.13.cloned.1.call-start = ((), (), s32[]{:S(2)}) async-start(), calls=%async_computation.8 | async-start | bytes 589824
  15.6 2.4 copy-start.4
  15.6 119.4 %copy-start.3 = (bf16[2,4,2,64,64]{4,3,2,1,0:T(8,128)(2,1)S(1)}, bf16[2,4,2,64,64]{4,3,2,1,0:T(8,128)(2,1)}, u32[]{:S(2)}) copy-start(bf16[2,4,2,64,64]{4,3,2,1,0:T(8,128)(2,1)} %param.7) | copy-start | bytes 393220
  18.0 241.2 %all-gather.3.cloned.1.call-start = ((), (), s32[]{:S(2)}) async-start(), calls=%async_computation.5 | async-start | bytes 2162688 | tf_op jit(solution)/shard_map/all_gather | solution.py:78
  134.9 255.9 %reduce-scatter.11.cloned.1.call-start = ((), (), s32[]{:S(2)}) async-start(), calls=%async_computation.6 | async-start | bytes 2162688 | tf_op jit(solution)/shard_map/reduce_scatter | solution.py:57
  201.0 62.9 %copy-start.5 = (bf16[2,256,64]{1,2,0:T(8,128)(2,1)S(1)}, bf16[2,256,64]{1,2,0:T(8,128)(2,1)}, u32[]{:S(2)}) copy-start(bf16[2,256,64]{1,2,0:T(8,128)(2,1)} %param.9) | copy-start | bytes 196612
  201.0 62.9 %copy-start.7 = (bf16[2,64,256]{2,1,0:T(8,128)(2,1)S(1)}, bf16[2,64,256]{2,1,0:T(8,128)(2,1)}, u32[]{:S(2)}) copy-start(bf16[2,64,256]{2,1,0:T(8,128)(2,1)} %param.8) | copy-start | bytes 196612
  276.1 4.6 copy-start.1
  280.4 151.3 %reduce-scatter.15.cloned.1.call-start = ((), (), s32[]{:S(2)}) async-start(), calls=%async_computation.9 | async-start | bytes 589824
  283.3 107.5 %copy-start.2 = (bf16[1,2,64,64]{3,2,1,0:T(8,128)(2,1)S(1)}, bf16[1,2,64,64]{3,2,1,0:T(8,128)(2,1)}, u32[]{:S(2)}) copy-start(bf16[1,2,64,64]{3,2,1,0:T(8,128)(2,1)} %get-tuple-element.7) | copy-start | bytes 49156
  285.6 233.0 %all-gather.5.cloned.1.call-start = ((), (), s32[]{:S(2)}) async-start(), calls=%async_computation.7 | async-start | bytes 2162688 | tf_op jit(solution)/shard_map/all_gather | solution.py:78
  460.5 62.9 %copy-start.6 = (bf16[2,256,64]{1,2,0:T(8,128)(2,1)S(1)}, bf16[2,256,64]{1,2,0:T(8,128)(2,1)}, u32[]{:S(2)}) copy-start(bf16[2,256,64]{1,2,0:T(8,128)(2,1)} %param.9) | copy-start | bytes 196612
  460.5 62.9 %copy-start.8 = (bf16[2,64,256]{2,1,0:T(8,128)(2,1)S(1)}, bf16[2,64,256]{2,1,0:T(8,128)(2,1)}, u32[]{:S(2)}) copy-start(bf16[2,64,256]{2,1,0:T(8,128)(2,1)} %param.8) | copy-start | bytes 196612
Sparse Core Ops, SparseCore 0:
  13.1 117.6 reduce-scatter.8
  133.4 38.6 reduce-scatter.12
  174.8 84.2 all-gather.2
  280.5 110.2 reduce-scatter.10
  393.4 38.2 reduce-scatter.14
  434.3 84.2 all-gather.4
where the time goes:
time: 545 us; the launch traced here: 544 us
  waiting for transfers between devices  404 us (74%)
  matrix products  51.9 us (10%)
  blocking collectives  48.2 us (9%)
  local copies, waits for them, and re-layouts  20.5 us (4%)
  between operations  13.8 us (3%)
    reduce_scatter x2, waiting for transfers between devices, body(): lax.psum_scatter(jnp.einsum('kx,zcxy->kzcy', forward_xloc, state, preferr...  217 us
    all_gather x2, waiting for transfers between devices, body(): lax.all_gather(mixed_x, 'gx', axis=0, tiled=True)  116 us
    unnamed x8, waiting for transfers between devices  70.6 us
    all_gather x2, blocking collectives, body(): lax.all_gather(mixed_y, 'gy', axis=0, tiled=True)  48.2 us
    dot_general x2, matrix products, body(): jnp.einsum('hc,zhxy->zcxy', reduce_weight[layer_index], hidden, preferred...  23 us
  transfers between devices with their start and end apart: 6, of which 6 were waited for; matrix products, arithmetic and copies ran while one was open for 5% of the time, Pallas kernels for 0%

commit v1 on v0

--- a/solution.py
+++ b/solution.py
@@ -75,7 +75,9 @@
         branch_x = jnp.einsum(
             "xk,kzcy->zcxy",
             inverse_xloc,
-            lax.all_gather(mixed_x, "gx", axis=0, tiled=True),
+            jnp.concatenate(
+                lax.all_to_all(jnp.stack([mixed_x] * lax.axis_size("gx")), "gx", 0, 0), axis=0
+            ),
             preferred_element_type=jnp.float32,
         ).astype(jnp.bfloat16)
         branch_y = jnp.einsum(

time: 545 us -> 520 us (0.954)
  the two profiles are of different devices: /device:TPU:1 before, /device:TPU:32 now
where the time goes in v1:
time: 520 us; the launch traced here: 511 us
  waiting for transfers between devices  321 us (62%)
  blocking collectives  61.5 us (12%)
  matrix products  50.2 us (10%)
  local copies, waits for them, and re-layouts  45.3 us (9%)
  between operations  15.4 us (3%)
  starting transfers between devices  14.7 us (3%)
    reduce_scatter x2, waiting for transfers between devices, body(): lax.psum_scatter(jnp.einsum('kx,zcxy->kzcy', forward_xloc, state, preferr...  236 us
    unnamed x6, waiting for transfers between devices  84.6 us
    all_gather x2, blocking collectives, body(): lax.all_gather(mixed_y, 'gy', axis=0, tiled=True)  61.5 us
    dot_general x2, matrix products, body(): jnp.einsum('hc,zhxy->zcxy', reduce_weight[layer_index], hidden, preferred...  23.2 us
    all_to_all x2, starting transfers between devices, body(): lax.all_to_all(jnp.stack([mixed_x] * lax.axis_size('gx')), 'gx', 0, 0)  14.5 us
    all_to_all x2, local copies, waits for them, and re-layouts, body(): lax.all_to_all(jnp.stack([mixed_x] * lax.axis_size('gx')), 'gx', 0, 0)  10.4 us
  transfers between devices with their start and end apart: 6, of which 4 were waited for; matrix products, arithmetic and copies ran while one was open for 4% of the time, Pallas kernels for 0%

profile of v1, /device:TPU:32, one launch (start us, length us, event | category | flops | bytes accessed | tf_op | source)
XLA Modules:
  0.0 511.1 jit_solution(12090558792914323973)
XLA Ops:
  7.4 1.1 multiply_convert_fusion.2
  8.9 2.3 convert_bitcast_fusion.3
  11.2 2.5 copy.130
  13.8 0.8 copy-done.4
  15.2 119.7 %reduce-scatter.9.cloned.1.call-done = bf16[2,1,64,256]{3,2,1,0:T(8,128)(2,1)} async-done(((bf16[64,1,64,256]{3,2,1,0:T(8,128)(2,1)}), bf16[2,1,64,256]{3,2,1,0:T(8,128)(2,1)}) %reduce-scatter.9.cloned.1.call-update) | async-done | bytes 65552 | tf_op jit(solution)/shard_map/reduce_scatter | solution.py:57
  134.9 0.9 fusion.108
  135.8 0.9 fusion.107
  136.6 0.9 fusion.73
  137.5 0.9 fusion.74
  138.5 3.2 stack.64
  141.7 7.3 %all-to-all-start = ((bf16[32,2,1,64,256]{4,1,3,2,0:T(2,128)(2,1)}), bf16[32,2,1,64,256]{4,1,3,2,0:T(2,128)(2,1)}, u32[]{:S(2)}, u32[]{:S(2)}) async-start(bf16[32,2,1,64,256]{4,1,3,2,0:T(2,128)(2,1)} %stack.64), calls=%async_computation.1 | async-start | bytes 4194304 | tf_op jit(solution)/shard_map/all_to_all | solution.py:79
  149.1 1.1 fusion.53
  150.3 0.7 copy.161
  151.0 1.6 reshape.470
  152.7 1.0 multiply_convert_fusion
  153.7 1.0 multiply_convert_fusion.1
  155.0 0.8 convert_element_type.181
  155.8 40.6 %reduce-scatter.13.cloned.1.call-done = bf16[8,4096]{1,0:T(8,128)(2,1)} async-done(((bf16[64,4096]{1,0:T(8,128)(2,1)}), bf16[8,4096]{1,0:T(8,128)(2,1)}) %reduce-scatter.13.cloned.1.call-update) | async-done | bytes 65552
  196.4 1.0 reshape.471
  198.5 31.0 %all_gather.6 = bf16[64,1,64,64]{3,2,1,0:T(8,128)(2,1)S(1)} all-gather(bf16[8,1,64,64]{3,2,1,0:T(8,128)(2,1)S(1)} %bitcast.310), channel_id=1, replica_groups=mesh['gx'=32,'gy'=8] {'gy'}, dimensions={0}, use_global_device_ids=true | all-gather | bytes 589824 | tf_op jit(solution)/shard_map/all_gather | solution.py:86
  229.4 1.2 copy.141
  230.7 1.4 fusion.77
  232.1 5.2 %copy.132 = bf16[32,2,1,64,256]{4,1,0,3,2:T(2,128)(2,1)} copy(bf16[32,2,1,64,256]{4,1,3,2,0:T(2,128)(2,1)} %all-to-all-done) | data formatting | bytes 4194304 | tf_op jit(solution)/shard_map/all_to_all | solution.py:79
  237.3 4.1 reshape.438
  241.5 3.8 fusion.24
  245.2 12.4 %fusion.22 = bf16[1,64,64,256]{3,1,2,0:T(8,128)(2,1)S(1)} fusion(bf16[1,64,64,256]{3,2,1,0:T(8,128)(2,1)} %param.5, bf16[64,64,256]{2,1,0:T(8,128)(2,1)} %fusion.24, bf16[2,256,64]{1,2,0:T(8,128)(2,1)S(1)} %copy-done.5, bf16[2,64,256]{2,1,0:T(8,128)(2,1)S(1)} %copy-done.7), kind=kOutput, calls=%fused_computation.28 | convolution fusion | flops 1114636288 | bytes 6356992 | tf_op jit(solution)/shard_map/hc,zhxy->zcxy/dot_general | solution.py:100
  257.6 1.7 convert_bitcast_fusion.2
  259.4 2.5 copy.145
  262.0 116.6 %reduce-scatter.11.cloned.1.call-done = bf16[2,1,64,256]{3,2,1,0:T(8,128)(2,1)} async-done(((bf16[64,1,64,256]{3,2,1,0:T(8,128)(2,1)}), bf16[2,1,64,256]{3,2,1,0:T(8,128)(2,1)}) %reduce-scatter.11.cloned.1.call-update) | async-done | bytes 65552 | tf_op jit(solution)/shard_map/reduce_scatter | solution.py:57
  378.6 0.9 fusion.109
  379.5 0.9 fusion.110
  380.4 0.9 fusion.72
  381.2 0.9 fusion.71
  382.2 3.2 stack.72
  385.4 7.2 %all-to-all-start.1 = ((bf16[32,2,1,64,256]{4,1,3,2,0:T(2,128)(2,1)}), bf16[32,2,1,64,256]{4,1,3,2,0:T(2,128)(2,1)}, u32[]{:S(2)}, u32[]{:S(2)}) async-start(bf16[32,2,1,64,256]{4,1,3,2,0:T(2,128)(2,1)} %stack.72), calls=%async_computation.3 | async-start | bytes 4194304 | tf_op jit(solution)/shard_map/all_to_all | solution.py:79
  392.7 2.6 fusion.56
  395.3 0.7 copy.163
  396.0 1.6 reshape.472
  397.7 44.0 %reduce-scatter.15.cloned.1.call-done = bf16[8,4096]{1,0:T(8,128)(2,1)} async-done(((bf16[64,4096]{1,0:T(8,128)(2,1)}), bf16[8,4096]{1,0:T(8,128)(2,1)}) %reduce-scatter.15.cloned.1.call-update) | async-done | bytes 65552
  441.6 1.0 reshape.473
  443.7 30.5 %all_gather.7 = bf16[64,1,64,64]{3,2,1,0:T(8,128)(2,1)S(1)} all-gather(bf16[8,1,64,64]{3,2,1,0:T(8,128)(2,1)S(1)} %bitcast.311), channel_id=1, replica_groups=mesh['gx'=32,'gy'=8] {'gy'}, dimensions={0}, use_global_device_ids=true | all-gather | bytes 589824 | tf_op jit(solution)/shard_map/all_gather | solution.py:86
  474.2 1.4 copy.155
  475.6 1.4 fusion.75
  477.1 5.2 %copy.147 = bf16[32,2,1,64,256]{4,1,0,3,2:T(2,128)(2,1)} copy(bf16[32,2,1,64,256]{4,1,3,2,0:T(2,128)(2,1)} %all-to-all-done.1) | data formatting | bytes 4194304 | tf_op jit(solution)/shard_map/all_to_all | solution.py:79
  482.3 4.1 reshape.451
  486.4 3.8 fusion.25
  490.2 10.8 %fusion.20 = bf16[1,64,64,256]{3,1,2,0:T(8,128)(2,1)S(1)} fusion(bf16[1,64,64,256]{3,1,2,0:T(8,128)(2,1)} %copy-done.1, bf16[64,64,256]{2,1,0:T(8,128)(2,1)} %fusion.25, bf16[2,256,64]{1,2,0:T(8,128)(2,1)S(1)} %copy-done.6, bf16[2,64,256]{2,1,0:T(8,128)(2,1)S(1)} %copy-done.8), kind=kOutput, calls=%fused_computation.23 | convolution fusion | flops 1114636288 | bytes 6356992 | tf_op jit(solution)/shard_map/hc,zhxy->zcxy/dot_general | solution.py:100
  501.0 2.5 copy.158
  (53 shorter events, 3.8 us)
Async XLA Ops:
  7.4 127.5 %reduce-scatter.9.cloned.1.call-start = ((), (), s32[]{:S(2)}) async-start(), calls=%async_computation.6 | async-start | bytes 2162688 | tf_op jit(solution)/shard_map/reduce_scatter | solution.py:57
  13.7 0.8 copy-start.4
  141.7 7.4 %copy-start = (bf16[1,64,64,256]{3,2,1,0:T(8,128)(2,1)S(1)}, bf16[1,64,64,256]{3,2,1,0:T(8,128)(2,1)}, u32[]{:S(2)}) copy-start(bf16[1,64,64,256]{3,2,1,0:T(8,128)(2,1)} %param.5) | copy-start | bytes 6291460
  141.7 90.4 %all-to-all-start = ((bf16[32,2,1,64,256]{4,1,3,2,0:T(2,128)(2,1)}), bf16[32,2,1,64,256]{4,1,3,2,0:T(2,128)(2,1)}, u32[]{:S(2)}, u32[]{:S(2)}) async-start(bf16[32,2,1,64,256]{4,1,3,2,0:T(2,128)(2,1)} %stack.64), calls=%async_computation.1 | async-start | bytes 4194304 | tf_op jit(solution)/shard_map/all_to_all | solution.py:79
  149.1 47.3 %reduce-scatter.13.cloned.1.call-start = ((), (), s32[]{:S(2)}) async-start(), calls=%async_computation.8 | async-start | bytes 589824
  150.3 2.4 copy-start.3
  152.6 226.0 %reduce-scatter.11.cloned.1.call-start = ((), (), s32[]{:S(2)}) async-start(), calls=%async_computation.7 | async-start | bytes 2162688 | tf_op jit(solution)/shard_map/reduce_scatter | solution.py:57
  241.4 3.8 copy-start.5
  241.4 3.8 copy-start.7
  257.6 135.1 %copy-start.1 = (bf16[1,64,64,256]{3,1,2,0:T(8,128)(2,1)}, bf16[1,64,64,256]{3,1,2,0:T(8,128)(2,1)S(1)}, u32[]{:S(2)}) copy-start(bf16[1,64,64,256]{3,1,2,0:T(8,128)(2,1)S(1)} %fusion.22) | copy-start | bytes 6291460
  261.9 116.7 %copy-start.2 = (bf16[1,2,64,64]{3,2,1,0:T(8,128)(2,1)S(1)}, bf16[1,2,64,64]{3,2,1,0:T(8,128)(2,1)}, u32[]{:S(2)}) copy-start(bf16[1,2,64,64]{3,2,1,0:T(8,128)(2,1)} %get-tuple-element.7) | copy-start | bytes 49156
  385.4 91.6 %all-to-all-start.1 = ((bf16[32,2,1,64,256]{4,1,3,2,0:T(2,128)(2,1)}), bf16[32,2,1,64,256]{4,1,3,2,0:T(2,128)(2,1)}, u32[]{:S(2)}, u32[]{:S(2)}) async-start(bf16[32,2,1,64,256]{4,1,3,2,0:T(2,128)(2,1)} %stack.72), calls=%async_computation.3 | async-start | bytes 4194304 | tf_op jit(solution)/shard_map/all_to_all | solution.py:79
  392.6 49.0 %reduce-scatter.15.cloned.1.call-start = ((), (), s32[]{:S(2)}) async-start(), calls=%async_computation.9 | async-start | bytes 589824
  486.4 3.8 copy-start.6
  486.4 3.8 copy-start.8
Sparse Core Ops, SparseCore 0:
  13.9 120.9 reduce-scatter.8
  262.1 116.4 reduce-scatter.10
Sparse Core Ops, SparseCore 1:
  152.7 43.6 reduce-scatter.12
  397.7 43.8 reduce-scatter.14
